TPU v7x, 32 devices: a whole 2x2x4 slice. The times are simulated.
32 devices in a mesh: group: 2 (over y), ctx: 4 (over z), head: 2 (over x), req: 2 (over core).
Axes of the slice: x: 2, y: 2, z: 4, core: 2. Of those that a mesh axis runs over, the one named last changes fastest.
Arguments:
- kda_query: bfloat16 [4, 768, 4096], P(('group', 'req'), 'ctx', 'head'), parts along dimension 0, may hold values from -6 to 6
- kda_key: bfloat16 [4, 768, 4096], P(('group', 'req'), 'ctx', 'head'), parts along dimension 0, may hold values from -6 to 6
- kda_value: bfloat16 [4, 768, 4096], P(('group', 'req'), 'ctx', 'head'), parts along dimension 0, may hold values from -6 to 6
- log_decay: bfloat16 [4, 768, 4096], P(('group', 'req'), 'ctx', 'head'), parts along dimension 0, may hold values from -1 to 0
- write_strength: float32 [4, 32, 768], P(('group', 'req'), 'head', 'ctx'), parts along dimension 0, may hold values from 0.1 to 0.95
- mla_query: bfloat16 [4, 768, 18432], P(('group', 'req'), 'ctx', 'head'), parts along dimension 0, may hold values from -18 to 18
- latents: bfloat16 [4, 768, 576], P(('group', 'req'), 'ctx'), parts along dimension 0, may hold values from -8 to 8
- value_up: bfloat16 [32, 512, 128], P('head'), may hold values from -0.25 to 0.25
- out_proj: bfloat16 [4096, 2304], P('head'), may hold values from -0.09375 to 0.09375
- doc_lengths: int32 [4, 8], P(('group', 'req')), parts along dimension 0, may hold values from 1 to 288, 768 in all within a row
Outputs:
- kda_out: bfloat16 [4, 768, 4096], P(('group', 'req'), 'ctx', 'head'), parts along dimension 0
- mixed: bfloat16 [4, 768, 2304], P(('group', 'req'), ('ctx', 'head')), parts along dimension 0
There are 2 independent parts, one for each index of `group`. A program takes and returns all parts, laid end to end along the dimension named above; an argument that names none is the same for every part. Nothing has to cross between parts.
Inputs may be any that keep to these rules, and one draw needn't show every extreme that they name: `doc_lengths`: each row's lengths sum to 768, and each row's longest prompt has exactly 288 positions.
All inputs are finite; a program needn't handle non-finite values.
Results may differ from a plain program's by a relative error of at most 0.009.
Values may be sent and summed in bfloat16 or wider, within the bound.
A program may use at most 128 MiB of HBM per device.

v0:
```python
import math
import jax
import jax.numpy as jnp
from jax import lax
from jax.sharding import PartitionSpec as P

ROPE = 64
NOPE = 128
SPAN = 64
top_value = lax.Precision.HIGHEST
masked_score = -1e30


def from_behind(value, axis, by):
    peers = lax.axis_size(axis)
    pairs = [(i, i + by) for i in range(peers) if 0 <= i + by < peers]
    return lax.ppermute(value, axis, pairs)


def unit_length(values):
    return values * lax.rsqrt(jnp.sum(values * values, axis=-1, keepdims=True) + 1e-06)


def doc_index(position_list, doc_ends):
    return jnp.sum((doc_ends[None, :] <= position_list[:, None]).astype(jnp.int32), axis=1)


def span_terms(query_rows, key_rows, value_rows, decay_rows, strength, doc_ids, prev_doc):
    span_len = key_rows.shape[1]
    state_dim = key_rows.shape[2]
    row_index = jnp.arange(span_len, dtype=jnp.int32)
    inclusive = (row_index[:, None] >= row_index[None, :]).astype(jnp.float32)
    summed = jnp.einsum("ij,hjc->hic", inclusive, decay_rows, precision=top_value)
    growth = jnp.exp(summed)
    key_hat = key_rows * growth
    key_tilde = key_rows * jnp.exp(-summed)
    query_estimate = query_rows * growth
    same_doc = doc_ids[:, None] == doc_ids[None, :]
    strict = same_doc & (row_index[:, None] > row_index[None, :])
    up_to = same_doc & (row_index[:, None] >= row_index[None, :])
    carried = (doc_ids == prev_doc).astype(jnp.float32)
    inner = jnp.einsum("hic,hjc->hij", key_hat, key_tilde, precision=top_value)
    lower_part = jnp.where(strict[None], inner * strength[:, :, None], 0.0)
    system = lower_part + jnp.eye(span_len, dtype=jnp.float32)[None]
    right_side = jnp.concatenate(
        [(strength * carried[None])[:, :, None] * key_hat, strength[:, :, None] * value_rows],
        axis=2,
    )
    solved = lax.linalg.triangular_solve(
        system, right_side, left_side=True, lower=True, unit_diagonal=True
    )
    weighted_key_rows = solved[:, :, :state_dim]
    update_rows = solved[:, :, state_dim:]
    attend = jnp.where(
        up_to[None], jnp.einsum("hic,hjc->hij", query_estimate, key_tilde, precision=top_value), 0.0
    )
    tail_mask = same_doc[span_len - 1].astype(jnp.float32)
    key_decay = key_rows * jnp.exp(summed[:, span_len - 1 :, :] - summed) * tail_mask[None, :, None]
    diagonal = (
        carried[span_len - 1]
        * growth[:, span_len - 1, :, None]
        * jnp.eye(state_dim, dtype=jnp.float32)[None]
    )
    transition = diagonal - jnp.einsum(
        "hjc,hjd->hcd", key_decay, weighted_key_rows, precision=top_value
    )
    offset = jnp.einsum("hjc,hjv->hcv", key_decay, update_rows, precision=top_value)
    return (query_estimate, carried, weighted_key_rows, update_rows, attend, transition, offset)


def span_output(terms, inbound_state):
    query_estimate, carried, weighted_key_rows, update_rows, attend, transition, offset = terms
    adjusted_rows = update_rows - jnp.einsum(
        "izy,iyn->izn", weighted_key_rows, inbound_state, precision=top_value
    )
    state_contribution = jnp.einsum(
        "izy,iyn->izn", query_estimate, inbound_state, precision=top_value
    )
    return carried[None, :, None] * state_contribution + jnp.einsum(
        "hij,hjv->hiv", attend, adjusted_rows, precision=top_value
    )


def apply_map(transition, offset, inbound_state):
    return jnp.einsum("hcd,hdv->hcv", transition, inbound_state, precision=top_value) + offset


def local(
    kda_query,
    kda_key,
    kda_value,
    log_decay,
    write_strength,
    mla_query,
    latents,
    value_up,
    out_proj,
    doc_lengths,
):
    tokens_dev = kda_query.shape[1]
    heads_dev = write_strength.shape[1]
    state_dim = kda_query.shape[2] // heads_dev
    ctx_count = lax.axis_size("ctx")
    ctx_place = lax.axis_index("ctx")
    first_pos = ctx_place * tokens_dev
    positions = first_pos + jnp.arange(tokens_dev, dtype=jnp.int32)
    doc_ends = jnp.cumsum(doc_lengths[0])
    doc_ids = doc_index(positions, doc_ends)

    def head_first(packed):
        return jnp.transpose(
            packed[0].astype(jnp.float32).reshape(tokens_dev, heads_dev, state_dim), (1, 0, 2)
        )

    query_rows = unit_length(head_first(kda_query))
    key_rows = unit_length(head_first(kda_key))
    value_rows = head_first(kda_value)
    decay_rows = head_first(log_decay)
    strength = write_strength[0]
    span_list = []
    eye_batch = jnp.broadcast_to(
        jnp.eye(state_dim, dtype=jnp.float32), (heads_dev, state_dim, state_dim)
    )
    transition = eye_batch
    offset = jnp.zeros((heads_dev, state_dim, state_dim), jnp.float32)
    for span_begin in range(0, tokens_dev, SPAN):
        span_stop = span_begin + SPAN
        prev_doc = doc_index(positions[span_begin : span_begin + 1] - 1, doc_ends)[0]
        terms = span_terms(
            query_rows[:, span_begin:span_stop],
            key_rows[:, span_begin:span_stop],
            value_rows[:, span_begin:span_stop],
            decay_rows[:, span_begin:span_stop],
            strength[:, span_begin:span_stop],
            doc_ids[span_begin:span_stop],
            prev_doc,
        )
        span_list.append(terms)
        offset = apply_map(terms[5], terms[6], offset)
        transition = jnp.einsum("hcd,hde->hce", terms[5], transition, precision=top_value)

    def relay(turn_index, inbound_state):
        outgoing = apply_map(transition, offset, inbound_state)
        return from_behind(outgoing.astype(jnp.bfloat16), "ctx", 1).astype(outgoing.dtype)

    inbound_state = lax.fori_loop(0, ctx_count - 1, relay, jnp.zeros_like(offset))
    pieces = []
    state_now = inbound_state
    for span_number, terms in enumerate(span_list):
        pieces.append(span_output(terms, state_now))
        if span_number + 1 < len(span_list):
            state_now = apply_map(terms[5], terms[6], state_now)
    kda_out = (
        jnp.transpose(jnp.concatenate(pieces, axis=1), (1, 0, 2))
        .reshape(1, tokens_dev, heads_dev * state_dim)
        .astype(jnp.bfloat16)
    )
    width = latents.shape[2]
    lat_dim = value_up.shape[1]
    score_scale = 1.0 / math.sqrt(NOPE + ROPE)
    query_flat = mla_query[0].reshape(tokens_dev * heads_dev, width)
    row_pos = jnp.repeat(positions, heads_dev)
    row_doc = jnp.repeat(doc_ids, heads_dev)
    row_total_count = tokens_dev * heads_dev
    row_peak = jnp.full((row_total_count,), masked_score, jnp.float32)
    block_rows = lax.all_gather(latents, "ctx", axis=1, tiled=True)[0]
    row_count = block_rows.shape[0]
    key_pos = jnp.arange(row_count, dtype=jnp.int32)
    key_doc = doc_index(key_pos, doc_ends)
    scores = (
        lax.dot_general(
            query_flat, block_rows, (((1,), (1,)), ((), ())), preferred_element_type=jnp.float32
        )
        * score_scale
    )
    allowed = (
        (key_pos[None, :] <= row_pos[:, None])
        & (key_pos[None, :] >= 0)
        & (key_doc[None, :] == row_doc[:, None])
    )
    new_peak = jnp.maximum(row_peak, jnp.max(jnp.where(allowed, scores, masked_score), axis=1))
    exponent = jnp.where(allowed, jnp.exp(scores - new_peak[:, None]), 0.0)
    row_total = jnp.sum(exponent, axis=1)
    weighted = jnp.dot(
        exponent.astype(jnp.bfloat16), block_rows[:, :lat_dim], preferred_element_type=jnp.float32
    )
    row_peak, row_total, weighted = (new_peak, row_total, weighted)
    context = (
        (weighted / row_total[:, None]).astype(jnp.bfloat16).reshape(tokens_dev, heads_dev, lat_dim)
    )
    head_out = jnp.einsum(
        "thl,hlv->thv", context, value_up, preferred_element_type=jnp.float32
    ).astype(jnp.bfloat16)
    head_out = head_out.reshape(tokens_dev, heads_dev * value_up.shape[2])
    mixed = lax.psum_scatter(
        jnp.dot(head_out, out_proj, preferred_element_type=jnp.float32).astype(jnp.bfloat16),
        "head",
        scatter_dimension=0,
        tiled=True,
    )
    return (kda_out, mixed[None])


def solution(mesh):
    placed = (
        P(("group", "req"), "ctx", "head"),
        P(("group", "req"), "ctx", "head"),
        P(("group", "req"), "ctx", "head"),
        P(("group", "req"), "ctx", "head"),
        P(("group", "req"), "head", "ctx"),
        P(("group", "req"), "ctx", "head"),
        P(("group", "req"), "ctx", None),
        P("head", None, None),
        P("head", None),
        P(("group", "req"), None),
    )
    return jax.shard_map(
        local,
        mesh=mesh,
        in_specs=placed,
        out_specs=(P(("group", "req"), "ctx", "head"), P(("group", "req"), ("ctx", "head"), None)),
        check_vma=False,
    )
```

profile of v0, /device:TPU:0, one launch (start us, length us, event | category | flops | bytes accessed | tf_op | source)
XLA Modules:
  0.0 443.5 jit_solution(2530594987979370844)
XLA Ops:
  8.8 23.7 %all_gather.3 = bf16[1,768,576]{2,1,0:T(8,128)(2,1)S(1)} all-gather(bf16[1,192,576]{2,1,0:T(8,128)(2,1)} %param.20), channel_id=1, replica_groups=mesh['group'=2,'ctx'=4,'head'=2,'req'=2] {'ctx'}, dimensions={1}, use_global_device_ids=true | all-gather | bytes 1105920 | tf_op jit(solution)/shard_map/all_gather | solution.py:166
  32.5 7.0 %reshape_squeeze.3 = bf16[3072,576]{1,0:T(8,128)(2,1)} reshape(bf16[1,192,9216]{2,1,0:T(8,128)(2,1)} %param.19) | data formatting | bytes 7077888 | tf_op jit(solution)/shard_map/reshape;squeeze | solution.py:161
  39.4 6.7 %select_reduce_fusion = (f32[3072]{0:T(1024)S(1)}, f32[3072,768]{0,1:T(8,128)S(1)}) fusion(s32[3072]{0:T(1024)S(1)} %eq.140, s32[3072]{0:T(1024)S(1)} %le.114, s32[768]{0:T(1024)S(1)} %convert_reduce_fusion, bf16[3072,576]{1,0:T(8,128)(2,1)} %reshape_squeeze.3, bf16[1,768,576]{2,1,0:T(8,128)(2,1)S(1)} %all_gather.3), kind=kOutput, calls=%fused_computation.7 | convolution fusion | flops 2732061696 | bytes 13900800 | tf_op jit(solution)/shard_map/dot_general | solution.py:171
  46.2 3.6 fusion.6
  49.8 4.3 divide_convert_fusion
  54.2 3.7 fusion.20
  57.9 3.0 convolution_convert_fusion
  75.2 80.0 %custom-call.8 = f32[16,1,64,64]{2,3,1,0:T(8,128)} custom-call(f32[16,1,64,64]{3,2,1,0:T(8,128)} %fusion.30), custom_call_target="InvertDiagBlocksLowerTriangular" | custom-call | tf_op jit(solution)/shard_map/triangular_solve/custom-call.1 | solution.py:49
  157.8 2.8 broadcast_multiply_fusion.2
  174.3 80.2 %custom-call.7 = f32[16,1,64,64]{2,3,1,0:T(8,128)} custom-call(f32[16,1,64,64]{3,2,1,0:T(8,128)} %fusion.35), custom_call_target="InvertDiagBlocksLowerTriangular" | custom-call | tf_op jit(solution)/shard_map/triangular_solve/custom-call.1 | solution.py:49
  256.9 2.9 fusion.66
  259.8 3.1 convolution_subtract_fusion.1
  264.7 80.2 %custom-call.6 = f32[16,1,64,64]{2,3,1,0:T(8,128)} custom-call(f32[16,1,64,64]{3,2,1,0:T(8,128)} %fusion.40), custom_call_target="InvertDiagBlocksLowerTriangular" | custom-call | tf_op jit(solution)/shard_map/triangular_solve/custom-call.1 | solution.py:49
  346.4 3.1 convolution_add_fusion.4
  353.9 3.0 convolution_add_fusion.3
  360.2 53.5 %while.11 = (s32[]{:T(128)}, f32[16,128,128]{2,1,0:T(8,128)S(1)}, f32[16,128,128]{2,1,0:T(8,128)}, f32[16,128,128]{2,1,0:T(8,128)}, s32[]{:T(128)}, /*index=5*/s32[]{:T(128)}) while((s32[]{:T(128)}, f32[16,128,128]{2,1,0:T(8,128)S(1)}, f32[16,128,128]{2,1,0:T(8,128)}, f32[16,128,128]{2,1,0:T(8,128)}, s32[]{:T(128)}, ...), condition=%wide.region_8.10_spmd.clone, body=%wide.region_7.9_spmd.clone.sunk | while | flops 403701760 | bytes 7340151 | solution.py:146
  360.2 3.5 fusion.158
  366.5 9.6 %collective-permute-done = bf16[16,128,128]{2,1,0:T(8,128)(2,1)} collective-permute-done((bf16[16,128,128]{2,1,0:T(8,128)(2,1)}, bf16[16,128,128]{2,1,0:T(8,128)(2,1)}, u32[]{:S(2)}, u32[]{:S(2)}) %collective-permute-start) | collective-permute-done | bytes 524320 | tf_op jit(solution)/shard_map/while/body/eval_jaxpr/ppermute | solution.py:17
  377.3 3.5 fusion.158
  380.8 5.2 %collective-permute-start = (bf16[16,128,128]{2,1,0:T(8,128)(2,1)}, bf16[16,128,128]{2,1,0:T(8,128)(2,1)}, u32[]{:S(2)}, u32[]{:S(2)}) collective-permute-start(bf16[16,128,128]{2,1,0:T(8,128)(2,1)} %fusion.158), channel_id=1, source_target_pairs={{0,4},{4,8},{8,12},{1,5},{5,9},{9,13},{2,6},{6,10},{10,14},{3,7},{... | collective-permute-start | bytes 1572872 | tf_op jit(solution)/shard_map/while/body/eval_jaxpr/ppermute | solution.py:17
  385.9 8.7 %collective-permute-done = bf16[16,128,128]{2,1,0:T(8,128)(2,1)} collective-permute-done((bf16[16,128,128]{2,1,0:T(8,128)(2,1)}, bf16[16,128,128]{2,1,0:T(8,128)(2,1)}, u32[]{:S(2)}, u32[]{:S(2)}) %collective-permute-start) | collective-permute-done | bytes 524320 | tf_op jit(solution)/shard_map/while/body/eval_jaxpr/ppermute | solution.py:17
  395.8 3.5 fusion.158
  399.3 5.2 %collective-permute-start = (bf16[16,128,128]{2,1,0:T(8,128)(2,1)}, bf16[16,128,128]{2,1,0:T(8,128)(2,1)}, u32[]{:S(2)}, u32[]{:S(2)}) collective-permute-start(bf16[16,128,128]{2,1,0:T(8,128)(2,1)} %fusion.158), channel_id=1, source_target_pairs={{0,4},{4,8},{8,12},{1,5},{5,9},{9,13},{2,6},{6,10},{10,14},{3,7},{... | collective-permute-start | bytes 1572872 | tf_op jit(solution)/shard_map/while/body/eval_jaxpr/ppermute | solution.py:17
  404.5 7.8 %collective-permute-done = bf16[16,128,128]{2,1,0:T(8,128)(2,1)} collective-permute-done((bf16[16,128,128]{2,1,0:T(8,128)(2,1)}, bf16[16,128,128]{2,1,0:T(8,128)(2,1)}, u32[]{:S(2)}, u32[]{:S(2)}) %collective-permute-start) | collective-permute-done | bytes 524320 | tf_op jit(solution)/shard_map/while/body/eval_jaxpr/ppermute | solution.py:17
  (152 shorter events, 71.8 us)
Async XLA Ops:
  7.2 47.0 %copy-start = (bf16[16,512,128]{2,1,0:T(8,128)(2,1)S(1)}, bf16[16,512,128]{2,1,0:T(8,128)(2,1)}, u32[]{:S(2)}) copy-start(bf16[16,512,128]{2,1,0:T(8,128)(2,1)} %param.21) | copy-start | bytes 6291460
  7.2 428.9 %reduce-scatter.2.cloned.1.call-start = ((), (), s32[]{:S(2)}) async-start(), calls=%async_computation.1 | async-start | bytes 1327104 | tf_op jit(solution)/shard_map/reduce_scatter | solution.py:195
  46.2 11.7 %slice-start = ((s8[9437184]{0:T(1024)(128)(4,1)}), s8[4194304]{0:T(1024)(128)(4,1)S(1)}, s32[]{:S(2)}) async-start(s8[9437184]{0:T(1024)(128)(4,1)} %bitcast.155), calls=%async_computation.2 | async-start | bytes 8388608
  49.8 8.1 %slice-start.1 = ((s8[9437184]{0:T(1024)(128)(4,1)}), s8[4194304]{0:T(1024)(128)(4,1)S(1)}, s32[]{:S(2)}) async-start(s8[9437184]{0:T(1024)(128)(4,1)} %bitcast.155), calls=%async_computation.3 | async-start | bytes 8388608
  49.8 8.1 %slice-start.2 = ((s8[9437184]{0:T(1024)(128)(4,1)}), s8[1048576]{0:T(1024)(128)(4,1)S(1)}, s32[]{:S(2)}) async-start(s8[9437184]{0:T(1024)(128)(4,1)} %bitcast.155), calls=%async_computation.4 | async-start | bytes 2097152
  57.9 3.6 copy-start.24
  61.7 7.9 %copy-start.28 = (f32[1,16,192]{2,1,0:T(8,128)S(1)}, f32[1,16,192]{2,1,0:T(8,128)}, u32[]{:S(2)}) copy-start(f32[1,16,192]{2,1,0:T(8,128)} %param.18) | copy-start | bytes 36868
  163.1 5.3 %copy-start.15 = (f32[16,64,256]{2,1,0:T(8,128)}, f32[16,64,256]{2,1,0:T(8,128)S(1)}, u32[]{:S(2)}) copy-start(f32[16,64,256]{2,1,0:T(8,128)S(1)} %fusion.52) | copy-start | bytes 3145732
  165.0 5.4 %copy-start.12 = (f32[16,128,128]{2,1,0:T(8,128)}, f32[16,128,128]{2,1,0:T(8,128)S(1)}, u32[]{:S(2)}) copy-start(f32[16,128,128]{2,1,0:T(8,128)S(1)} %fusion.68) | copy-start | bytes 3145732
  168.4 4.0 copy-start.8
  256.9 6.0 %copy-start.16 = (f32[16,64,256]{2,1,0:T(8,128)}, f32[16,64,256]{2,1,0:T(8,128)S(1)}, u32[]{:S(2)}) copy-start(f32[16,64,256]{2,1,0:T(8,128)S(1)} %fusion.48) | copy-start | bytes 3145732
  259.8 3.1 copy-start.5
  346.3 3.2 copy-start.22
  346.3 3.2 copy-start.23
  346.4 3.2 copy-start.27
  350.6 3.2 copy-start.18
  353.8 3.0 copy-start.10
  353.8 3.0 copy-start.20
  363.7 12.4 %collective-permute-start = (bf16[16,128,128]{2,1,0:T(8,128)(2,1)}, bf16[16,128,128]{2,1,0:T(8,128)(2,1)}, u32[]{:S(2)}, u32[]{:S(2)}) collective-permute-start(bf16[16,128,128]{2,1,0:T(8,128)(2,1)} %fusion.158), channel_id=1, source_target_pairs={{0,4},{4,8},{8,12},{1,5},{5,9},{9,13},{2,6},{6,10},{10,14},{3,7},{... | collective-permute-start | bytes 1572872 | tf_op jit(solution)/shard_map/while/body/eval_jaxpr/ppermute | solution.py:17
  380.8 13.9 %collective-permute-start = (bf16[16,128,128]{2,1,0:T(8,128)(2,1)}, bf16[16,128,128]{2,1,0:T(8,128)(2,1)}, u32[]{:S(2)}, u32[]{:S(2)}) collective-permute-start(bf16[16,128,128]{2,1,0:T(8,128)(2,1)} %fusion.158), channel_id=1, source_target_pairs={{0,4},{4,8},{8,12},{1,5},{5,9},{9,13},{2,6},{6,10},{10,14},{3,7},{... | collective-permute-start | bytes 1572872 | tf_op jit(solution)/shard_map/while/body/eval_jaxpr/ppermute | solution.py:17
  399.3 13.0 %collective-permute-start = (bf16[16,128,128]{2,1,0:T(8,128)(2,1)}, bf16[16,128,128]{2,1,0:T(8,128)(2,1)}, u32[]{:S(2)}, u32[]{:S(2)}) collective-permute-start(bf16[16,128,128]{2,1,0:T(8,128)(2,1)} %fusion.158), channel_id=1, source_target_pairs={{0,4},{4,8},{8,12},{1,5},{5,9},{9,13},{2,6},{6,10},{10,14},{3,7},{... | collective-permute-start | bytes 1572872 | tf_op jit(solution)/shard_map/while/body/eval_jaxpr/ppermute | solution.py:17
  413.7 2.4 copy-start.9
  413.7 2.4 copy-start.13
  432.5 3.6 copy-start.1
  (12 other events, 14.9 us)
Sparse Core Ops, SparseCore 0:
  61.1 18.3 reduce-scatter.1
where the time goes:
time: 449 us; the launch traced here: 443 us
  other arithmetic  261 us (58%)
  matrix products  84.7 us (19%)
  waiting for transfers between devices  26.2 us (6%)
  blocking collectives  23.7 us (5%)
  between operations  17.1 us (4%)
  local copies, waits for them, and re-layouts  16.8 us (4%)
  starting transfers between devices  13.2 us (3%)
    another operation x5, other arithmetic, span_terms(): lax.linalg.triangular_solve(system, right_side, left_side=True, lower=Tru...  240 us
    ppermute x3, waiting for transfers between devices, from_behind(): return lax.ppermute(value, axis, pairs)  26.2 us
    all_gather x1, blocking collectives, local(): block_rows = lax.all_gather(latents, 'ctx', axis=1, tiled=True)[0]  23.7 us
    dot_general x8, matrix products, apply_map(): jnp.einsum('hcd,hdv->hcv', transition, inbound_state, precision=top_value)  19.1 us
    ppermute x3, starting transfers between devices, from_behind(): return lax.ppermute(value, axis, pairs)  13.1 us
  transfers between devices with their start and end apart: 4, of which 3 were waited for; matrix products, arithmetic and copies ran while one was open for 75% of the time, Pallas kernels for 0%

commit v1 on v0

--- a/solution.py
+++ b/solution.py
@@ -9,6 +9,28 @@
 SPAN = 64
 top_value = lax.Precision.HIGHEST
 masked_score = -1e30
+
+
+def joined_along(blocks, dim):
+    dims = list(blocks.shape[1:])
+    dims[dim] *= blocks.shape[0]
+    return jnp.moveaxis(blocks, 0, dim).reshape(dims)
+
+
+def collected_by_bits(x, axis):
+    count = lax.axis_size(axis)
+    parts = x[None]
+    for level in range(count.bit_length() - 1):
+        bit = 1 << level
+        received = lax.ppermute(parts, axis, [(i, i ^ bit) for i in range(count)])
+        both = jnp.stack([parts, received])
+        upper = lax.axis_index(axis) >> level & 1
+        parts = jnp.where(upper == 0, both, both[::-1]).reshape(-1, *x.shape)
+    return parts
+
+
+def collect(x, axis, dim):
+    return joined_along(collected_by_bits(x, axis), dim)
 
 
 def from_behind(value, axis, by):
@@ -163,7 +185,7 @@
     row_doc = jnp.repeat(doc_ids, heads_dev)
     row_total_count = tokens_dev * heads_dev
     row_peak = jnp.full((row_total_count,), masked_score, jnp.float32)
-    block_rows = lax.all_gather(latents, "ctx", axis=1, tiled=True)[0]
+    block_rows = collect(latents, "ctx", 1)[0]
     row_count = block_rows.shape[0]
     key_pos = jnp.arange(row_count, dtype=jnp.int32)
     key_doc = doc_index(key_pos, doc_ends)

time: 449 us -> 469 us (1.045)
  blocking collectives: 23.7 us -> 0 us
  waiting for transfers between devices: 26.2 us -> 42 us
  other arithmetic: 261 us -> 271 us
  matrix products: 84.7 us -> 93.8 us
  starting transfers between devices: 13.2 us -> 20.8 us
    all_gather x1 -> x0, blocking collectives: 23.7 us -> none  [local(): block_rows = lax.all_gather(latents, 'ctx', axis=1, tiled=True)[0]]
    ppermute x0 -> x2, starting transfers between devices: none -> 7.36 us  [collected_by_bits(): received = lax.ppermute(parts, axis, [(i, i ^ bit) for i in range(count)])]
    reduce_scatter x1, waiting for transfers between devices: 0.01 us -> 6.56 us  [local(): lax.psum_scatter(jnp.dot(head_out, out_proj, preferred_element_type=jnp.f...]
    ppermute x0 -> x2, waiting for transfers between devices: none -> 6.5 us  [collected_by_bits(): received = lax.ppermute(parts, axis, [(i, i ^ bit) for i in range(count)])]
    dot_general x3, matrix products: 3.13 us -> 8.48 us  [span_terms(): jnp.einsum('hic,hjc->hij', query_estimate, key_tilde, precision=top_value)]
  transfers between devices with their start and end apart: 4 -> 6, of which waited for: 3 -> 5; matrix products, arithmetic and copies ran while one was open for 75% -> 78% of each run, Pallas kernels for 0% -> 0%
where the time goes in v1:
time: 469 us; the launch traced here: 464 us
  other arithmetic  271 us (58%)
  matrix products  93.8 us (20%)
  waiting for transfers between devices  42 us (9%)
  starting transfers between devices  20.8 us (4%)
  local copies, waits for them, and re-layouts  19.4 us (4%)
  between operations  17.5 us (4%)
    another operation x5, other arithmetic, span_terms(): lax.linalg.triangular_solve(system, right_side, left_side=True, lower=Tru...  242 us
    ppermute x3, waiting for transfers between devices, from_behind(): return lax.ppermute(value, axis, pairs)  28.9 us
    dot_general x8, matrix products, apply_map(): jnp.einsum('hcd,hdv->hcv', transition, inbound_state, precision=top_value)  20.1 us
    ppermute x3, starting transfers between devices, from_behind(): return lax.ppermute(value, axis, pairs)  13.4 us
  transfers between devices with their start and end apart: 6, of which 5 were waited for; matrix products, arithmetic and copies ran while one was open for 78% of the time, Pallas kernels for 0%

profile of v1, /device:TPU:0, one launch (start us, length us, event | category | flops | bytes accessed | tf_op | source)
XLA Modules:
  0.0 464.3 jit_solution(9635688585772101428)
XLA Ops:
  7.2 3.1 collective-permute-start.1
  29.5 80.2 %custom-call.8 = f32[16,1,64,64]{2,3,1,0:T(8,128)} custom-call(f32[16,1,64,64]{3,2,1,0:T(8,128)} %fusion.33), custom_call_target="InvertDiagBlocksLowerTriangular" | custom-call | tf_op jit(solution)/shard_map/triangular_solve/custom-call.1 | solution.py:71
  129.8 80.2 %custom-call.7 = f32[16,1,64,64]{2,3,1,0:T(8,128)} custom-call(f32[16,1,64,64]{3,2,1,0:T(8,128)} %fusion.38), custom_call_target="InvertDiagBlocksLowerTriangular" | custom-call | tf_op jit(solution)/shard_map/triangular_solve/custom-call.1 | solution.py:71
  221.1 80.4 %custom-call.6 = f32[16,1,64,64]{2,3,1,0:T(8,128)} custom-call(f32[16,1,64,64]{3,2,1,0:T(8,128)} %fusion.43), custom_call_target="InvertDiagBlocksLowerTriangular" | custom-call | tf_op jit(solution)/shard_map/triangular_solve/custom-call.1 | solution.py:71
  303.7 3.1 convolution_add_fusion.4
  317.8 56.5 %while.11 = (s32[]{:T(128)}, f32[16,128,128]{2,1,0:T(8,128)S(1)}, f32[16,128,128]{2,1,0:T(8,128)}, f32[16,128,128]{2,1,0:T(8,128)}, s32[]{:T(128)}, /*index=5*/s32[]{:T(128)}) while((s32[]{:T(128)}, f32[16,128,128]{2,1,0:T(8,128)S(1)}, f32[16,128,128]{2,1,0:T(8,128)}, f32[16,128,128]{2,1,0:T(8,128)}, s32[]{:T(128)}, ...), condition=%wide.region_8.10_spmd.clone, body=%wide.region_7.9_spmd.clone.sunk | while | flops 403701760 | bytes 7340151 | solution.py:168
  317.8 3.5 fusion.162
  324.1 10.7 %collective-permute-done = bf16[16,128,128]{2,1,0:T(8,128)(2,1)} collective-permute-done((bf16[16,128,128]{2,1,0:T(8,128)(2,1)}, bf16[16,128,128]{2,1,0:T(8,128)(2,1)}, u32[]{:S(2)}, u32[]{:S(2)}) %collective-permute-start) | collective-permute-done | bytes 524320 | tf_op jit(solution)/shard_map/while/body/eval_jaxpr/ppermute | solution.py:39
  336.0 3.5 fusion.162
  339.5 5.4 %collective-permute-start = (bf16[16,128,128]{2,1,0:T(8,128)(2,1)}, bf16[16,128,128]{2,1,0:T(8,128)(2,1)}, u32[]{:S(2)}, u32[]{:S(2)}) collective-permute-start(bf16[16,128,128]{2,1,0:T(8,128)(2,1)} %fusion.162), channel_id=1, source_target_pairs={{0,4},{4,8},{8,12},{1,5},{5,9},{9,13},{2,6},{6,10},{10,14},{3,7},{... | collective-permute-start | bytes 1572872 | tf_op jit(solution)/shard_map/while/body/eval_jaxpr/ppermute | solution.py:39
  344.9 9.6 %collective-permute-done = bf16[16,128,128]{2,1,0:T(8,128)(2,1)} collective-permute-done((bf16[16,128,128]{2,1,0:T(8,128)(2,1)}, bf16[16,128,128]{2,1,0:T(8,128)(2,1)}, u32[]{:S(2)}, u32[]{:S(2)}) %collective-permute-start) | collective-permute-done | bytes 524320 | tf_op jit(solution)/shard_map/while/body/eval_jaxpr/ppermute | solution.py:39
  355.6 3.5 fusion.162
  359.1 5.2 %collective-permute-start = (bf16[16,128,128]{2,1,0:T(8,128)(2,1)}, bf16[16,128,128]{2,1,0:T(8,128)(2,1)}, u32[]{:S(2)}, u32[]{:S(2)}) collective-permute-start(bf16[16,128,128]{2,1,0:T(8,128)(2,1)} %fusion.162), channel_id=1, source_target_pairs={{0,4},{4,8},{8,12},{1,5},{5,9},{9,13},{2,6},{6,10},{10,14},{3,7},{... | collective-permute-start | bytes 1572872 | tf_op jit(solution)/shard_map/while/body/eval_jaxpr/ppermute | solution.py:39
  364.3 8.6 %collective-permute-done = bf16[16,128,128]{2,1,0:T(8,128)(2,1)} collective-permute-done((bf16[16,128,128]{2,1,0:T(8,128)(2,1)}, bf16[16,128,128]{2,1,0:T(8,128)(2,1)}, u32[]{:S(2)}, u32[]{:S(2)}) %collective-permute-start) | collective-permute-done | bytes 524320 | tf_op jit(solution)/shard_map/while/body/eval_jaxpr/ppermute | solution.py:39
  374.3 3.2 convolution_subtract_fusion.5
  392.6 4.3 collective-permute-start.2
  398.7 7.1 %reshape_squeeze.3 = bf16[3072,576]{1,0:T(8,128)(2,1)} reshape(bf16[1,192,9216]{2,1,0:T(8,128)(2,1)} %param.19) | data formatting | bytes 7077888 | tf_op jit(solution)/shard_map/reshape;squeeze | solution.py:183
  406.0 3.4 convolution_select_fusion.1
  409.4 6.5 %collective-permute-done.2 = bf16[2,1,192,576]{3,2,0,1:T(8,128)(2,1)} collective-permute-done((bf16[2,1,192,576]{3,2,0,1:T(8,128)(2,1)}, bf16[2,1,192,576]{3,2,0,1:T(8,128)(2,1)}, u32[]{:S(2)}, u32[]{:S(2)}) %collective-permute-start.2) | collective-permute-done | bytes 442400 | tf_op jit(solution)/shard_map/ppermute | solution.py:25
  418.1 4.6 fusion.5
  422.8 3.7 fusion.9
  426.4 4.3 divide_convert_fusion
  430.8 3.7 fusion.23
  450.4 6.6 %reduce-scatter.2.cloned.1.call-done = bf16[96,2304]{1,0:T(8,128)(2,1)} async-done(((bf16[192,2304]{1,0:T(8,128)(2,1)}), bf16[96,2304]{1,0:T(8,128)(2,1)}) %reduce-scatter.2.cloned.1.call-update) | async-done | bytes 442384 | tf_op jit(solution)/shard_map/reduce_scatter | solution.py:217
  (237 shorter events, 102.2 us)
Async XLA Ops:
  7.2 423.6 %copy-start = (bf16[16,512,128]{2,1,0:T(8,128)(2,1)S(1)}, bf16[16,512,128]{2,1,0:T(8,128)(2,1)}, u32[]{:S(2)}) copy-start(bf16[16,512,128]{2,1,0:T(8,128)(2,1)} %param.21) | copy-start | bytes 6291460
  7.2 449.8 %reduce-scatter.2.cloned.1.call-start = ((), (), s32[]{:S(2)}) async-start(), calls=%async_computation.1 | async-start | bytes 1327104 | tf_op jit(solution)/shard_map/reduce_scatter | solution.py:217
  7.2 384.2 %collective-permute-start.1 = (bf16[1,1,192,576]{3,2,1,0:T(8,128)(2,1)}, bf16[1,1,192,576]{3,2,1,0:T(8,128)(2,1)S(1)}, u32[]{:S(2)}, u32[]{:S(2)}) collective-permute-start(bf16[1,1,192,576]{3,2,1,0:T(8,128)(2,1)} %bitcast.165), channel_id=1, source_target_pairs={{0,4},{4,0},{8,12},{12,8},{1,5},{5,1},{9,13},{13,9},{2,6},{6,2},{1... | collective-permute-start | bytes 663560 | tf_op jit(solution)/shard_map/ppermute | solution.py:25
  11.6 5.5 %copy-start.67 = (s32[1,8]{1,0:T(1,128)S(1)}, s32[1,8]{1,0:T(1,128)}, u32[]{:S(2)}) copy-start(s32[1,8]{1,0:T(1,128)} %param.23) | copy-start | bytes 100
  11.6 10.2 %copy-start.45 = (f32[1,16,192]{2,1,0:T(8,128)S(1)}, f32[1,16,192]{2,1,0:T(8,128)}, u32[]{:S(2)}) copy-start(f32[1,16,192]{2,1,0:T(8,128)} %param.18) | copy-start | bytes 36868
  14.6 9.5 %copy-start.56 = (s32[192]{0:T(256)}, s32[192]{0:T(256)S(1)}, u32[]{:S(2)}) copy-start(s32[192]{0:T(256)S(1)} %iota_add_fusion) | copy-start | bytes 2308
  17.4 6.7 %copy-start.54 = (s32[192]{0:T(256)}, s32[192]{0:T(256)S(1)}, u32[]{:S(2)}) copy-start(s32[192]{0:T(256)S(1)} %convert_reduce_fusion.1) | copy-start | bytes 2308
  118.7 5.2 %copy-start.26 = (f32[16,64,256]{2,1,0:T(8,128)}, f32[16,64,256]{2,1,0:T(8,128)S(1)}, u32[]{:S(2)}) copy-start(f32[16,64,256]{2,1,0:T(8,128)S(1)} %fusion.55) | copy-start | bytes 3145732
  120.6 5.3 %copy-start.23 = (f32[16,128,128]{2,1,0:T(8,128)}, f32[16,128,128]{2,1,0:T(8,128)S(1)}, u32[]{:S(2)}) copy-start(f32[16,128,128]{2,1,0:T(8,128)S(1)} %fusion.71) | copy-start | bytes 3145732
  129.8 83.5 %copy-start.44 = (f32[16,1,128]{2,1,0:T(1,128)S(1)}, f32[16,1,128]{2,1,0:T(1,128)}, u32[]{:S(2)}) copy-start(f32[16,1,128]{2,1,0:T(1,128)} %slice.175) | copy-start | bytes 24580
  213.3 6.0 %copy-start.27 = (f32[16,64,256]{2,1,0:T(8,128)}, f32[16,64,256]{2,1,0:T(8,128)S(1)}, u32[]{:S(2)}) copy-start(f32[16,64,256]{2,1,0:T(8,128)S(1)} %fusion.51) | copy-start | bytes 3145732
  321.3 13.5 %collective-permute-start = (bf16[16,128,128]{2,1,0:T(8,128)(2,1)}, bf16[16,128,128]{2,1,0:T(8,128)(2,1)}, u32[]{:S(2)}, u32[]{:S(2)}) collective-permute-start(bf16[16,128,128]{2,1,0:T(8,128)(2,1)} %fusion.162), channel_id=1, source_target_pairs={{0,4},{4,8},{8,12},{1,5},{5,9},{9,13},{2,6},{6,10},{10,14},{3,7},{... | collective-permute-start | bytes 1572872 | tf_op jit(solution)/shard_map/while/body/eval_jaxpr/ppermute | solution.py:39
  339.5 15.0 %collective-permute-start = (bf16[16,128,128]{2,1,0:T(8,128)(2,1)}, bf16[16,128,128]{2,1,0:T(8,128)(2,1)}, u32[]{:S(2)}, u32[]{:S(2)}) collective-permute-start(bf16[16,128,128]{2,1,0:T(8,128)(2,1)} %fusion.162), channel_id=1, source_target_pairs={{0,4},{4,8},{8,12},{1,5},{5,9},{9,13},{2,6},{6,10},{10,14},{3,7},{... | collective-permute-start | bytes 1572872 | tf_op jit(solution)/shard_map/while/body/eval_jaxpr/ppermute | solution.py:39
  359.1 13.8 %collective-permute-start = (bf16[16,128,128]{2,1,0:T(8,128)(2,1)}, bf16[16,128,128]{2,1,0:T(8,128)(2,1)}, u32[]{:S(2)}, u32[]{:S(2)}) collective-permute-start(bf16[16,128,128]{2,1,0:T(8,128)(2,1)} %fusion.162), channel_id=1, source_target_pairs={{0,4},{4,8},{8,12},{1,5},{5,9},{9,13},{2,6},{6,10},{10,14},{3,7},{... | collective-permute-start | bytes 1572872 | tf_op jit(solution)/shard_map/while/body/eval_jaxpr/ppermute | solution.py:39
  391.4 5.5 %copy-start.37 = (f32[16,64,128]{2,1,0:T(8,128)S(1)}, f32[16,64,128]{2,1,0:T(8,128)}, u32[]{:S(2)}) copy-start(f32[16,64,128]{2,1,0:T(8,128)} %convolution_subtract_fusion.5) | copy-start | bytes 1572868
  391.5 6.8 %copy-start.55 = (s32[192]{0:T(256)S(1)}, s32[192]{0:T(256)}, u32[]{:S(2)}) copy-start(s32[192]{0:T(256)} %copy-done.54) | copy-start | bytes 2308
  391.5 7.0 %copy-start.57 = (s32[192]{0:T(256)S(1)}, s32[192]{0:T(256)}, u32[]{:S(2)}) copy-start(s32[192]{0:T(256)} %copy-done.56) | copy-start | bytes 2308
  392.6 23.3 %collective-permute-start.2 = (bf16[2,1,192,576]{3,2,0,1:T(8,128)(2,1)}, bf16[2,1,192,576]{3,2,0,1:T(8,128)(2,1)}, u32[]{:S(2)}, u32[]{:S(2)}) collective-permute-start(bf16[2,1,192,576]{3,2,0,1:T(8,128)(2,1)} %get-tuple-element.62), channel_id=1, source_target_pairs={{0,8},{4,12},{8,0},{12,4},{1,9},{5,13},{9,1},{13,5},{2,10},{6,14},... | collective-permute-start | bytes 1327112 | tf_op jit(solution)/shard_map/ppermute | solution.py:25
  398.7 7.2 %copy-start.65 = (s32[8,1]{0,1:T(1,128)S(1)}, s32[8,1]{0,1:T(1,128)}, u32[]{:S(2)}) copy-start(s32[8,1]{0,1:T(1,128)} %copy-done.64) | copy-start | bytes 100
  398.7 7.2 %copy-start.47 = (pred[64,64]{1,0:T(8,128)(4,1)S(1)}, pred[64,64]{1,0:T(8,128)(4,1)}, u32[]{:S(2)}) copy-start(pred[64,64]{1,0:T(8,128)(4,1)} %get-tuple-element.92) | copy-start | bytes 12292
  405.9 10.0 %copy-start.39 = (bf16[1,2,1,192,576]{4,3,1,2,0:T(8,128)(2,1)S(1)}, bf16[1,2,1,192,576]{4,3,1,2,0:T(8,128)(2,1)}, u32[]{:S(2)}) copy-start(bf16[1,2,1,192,576]{4,3,1,2,0:T(8,128)(2,1)} %get-tuple-element.61) | copy-start | bytes 1327108
  422.7 11.8 %slice-start = ((s8[9437184]{0:T(1024)(128)(4,1)}), s8[4194304]{0:T(1024)(128)(4,1)S(1)}, s32[]{:S(2)}) async-start(s8[9437184]{0:T(1024)(128)(4,1)} %bitcast.180), calls=%async_computation.2 | async-start | bytes 8388608
  426.4 8.1 %slice-start.1 = ((s8[9437184]{0:T(1024)(128)(4,1)}), s8[4194304]{0:T(1024)(128)(4,1)S(1)}, s32[]{:S(2)}) async-start(s8[9437184]{0:T(1024)(128)(4,1)} %bitcast.180), calls=%async_computation.3 | async-start | bytes 8388608
  426.4 8.1 %slice-start.2 = ((s8[9437184]{0:T(1024)(128)(4,1)}), s8[1048576]{0:T(1024)(128)(4,1)S(1)}, s32[]{:S(2)}) async-start(s8[9437184]{0:T(1024)(128)(4,1)} %bitcast.180), calls=%async_computation.4 | async-start | bytes 2097152
  (53 other events, 127.1 us)
Sparse Core Ops, SparseCore 0:
  437.8 19.1 reduce-scatter.1
